TPU v7x, 32 devices: a whole 2x2x4 slice. The times are simulated.
32 devices in a mesh: pairs: 2 (over y), blk: 8 (over z, x), panel: 2 (over core).
Axes of the slice: x: 2, y: 2, z: 4, core: 2. Of those that a mesh axis runs over, the one named last changes fastest.
Arguments:
- first_frame: bfloat16 [4096, 256], P(('pairs', 'blk', 'panel')), parts along dimension 0, may hold values from -8 to 8
- second_frame: bfloat16 [16, 8, 16, 256], P(('pairs', 'blk'), None, 'panel'), parts along dimension 0, may hold values from -8 to 8
Outputs:
- matched: float32 [4, 2, 4096], P(None, None, ('pairs', 'blk', 'panel')), parts along dimension 2
- energy: float32 [4, 4096], P(None, ('pairs', 'blk', 'panel')), parts along dimension 1
There are 2 independent parts, one for each index of `pairs`. A program takes and returns all parts, laid end to end along the dimension named above; each array names one. Nothing has to cross between parts.
All inputs are finite; a program needn't handle non-finite values.
Results may differ from a plain program's by a relative error of at most 0.014.
Values may be sent and summed in bfloat16 or wider, within the bound.
A program may use at most 128 MiB of HBM per device.

v0:
```python
import math
import jax
import jax.numpy as jnp
from jax import lax
from jax.sharding import PartitionSpec as P

LEVELS = 4
COLBLK = 8
BCOLS = 16
neg_large = -1e30


def build_levels(tile_batch):
    result = [tile_batch]
    pooled = tile_batch.astype(jnp.float32)
    for level_index in range(1, LEVELS):
        tile_count, height, columns, channels = pooled.shape
        pooled = pooled.reshape(tile_count, height // 2, 2, columns // 2, 2, channels).mean(
            axis=(2, 4)
        )
        result.append(pooled.astype(jnp.bfloat16))
    return result


def accumulate(carry_state, level_pieces, queries, col_start, total_rows, total_cols):
    maxima, totals = carry_state
    new_maxima = []
    new_totals = []
    for level_index in range(len(level_pieces)):
        level_piece = level_pieces[level_index]
        tile_count, height, columns, channels = level_piece.shape
        key_rows = level_piece.reshape(tile_count * height * columns, channels)
        factor = 3.0 * 2.0**level_index / math.sqrt(channels)
        scores = (
            jnp.einsum("kc,qc->kq", key_rows, queries, preferred_element_type=jnp.float32) * factor
        )
        merged_top = jnp.maximum(maxima[level_index], jnp.max(scores, axis=0))
        weights = jnp.exp(scores - merged_top[None, :])
        spacing = 2**level_index
        block_ids = jnp.arange(tile_count)
        row_index = (block_ids // COLBLK)[:, None, None] * height + jnp.arange(height)[
            None, :, None
        ]
        col_index = (
            (block_ids % COLBLK)[:, None, None] * (BCOLS // spacing)
            + col_start // spacing
            + jnp.arange(columns)[None, None, :]
        )
        row_grid = jnp.broadcast_to(row_index, (tile_count, height, columns)).astype(jnp.float32)
        col_grid = jnp.broadcast_to(col_index, (tile_count, height, columns)).astype(jnp.float32)
        row_pos = (row_grid + 0.5) * (float(spacing) / total_rows)
        col_pos = (col_grid + 0.5) * (float(spacing) / total_cols)
        unit_row = jnp.ones_like(row_pos)
        position_rows = jnp.stack([unit_row.reshape(-1), row_pos.reshape(-1), col_pos.reshape(-1)])
        block_totals = jnp.dot(
            position_rows,
            weights,
            precision=lax.Precision.HIGHEST,
            preferred_element_type=jnp.float32,
        )
        rescale = jnp.exp(maxima[level_index] - merged_top)
        new_totals.append(totals[level_index] * rescale[None, :] + block_totals)
        new_maxima.append(merged_top)
    return (jnp.stack(new_maxima), jnp.stack(new_totals))


def body(first_frame, second_frame):
    cycle_size = lax.axis_size("blk")
    panels = lax.axis_size("panel")
    block_count, tile_rows, tile_cols, channels = second_frame.shape
    total_rows = tile_rows * cycle_size // COLBLK
    total_cols = BCOLS * COLBLK
    col_start = lax.axis_index("panel") * tile_cols
    queries = lax.all_gather(first_frame, "panel", axis=0, tiled=True)
    query_count = queries.shape[0]
    init_state = (
        jnp.full((LEVELS, query_count), neg_large, jnp.float32),
        jnp.zeros((LEVELS, 3, query_count), jnp.float32),
    )
    level_zero, level_one, level_two, level_three = build_levels(second_frame)
    maxima, totals = accumulate(
        init_state,
        list(
            (
                lax.all_gather(level_zero, "blk", axis=0, tiled=True),
                lax.all_gather(level_one, "blk", axis=0, tiled=True),
                lax.all_gather(level_two, "blk", axis=0, tiled=True),
                lax.all_gather(level_three, "blk", axis=0, tiled=True),
            )
        ),
        queries,
        col_start,
        total_rows,
        total_cols,
    )
    half_count = query_count // panels
    own_max, own_tot = (
        lax.all_to_all(
            maxima.reshape(LEVELS, 1, panels, half_count),
            "panel",
            split_axis=2,
            concat_axis=2,
            tiled=True,
        ),
        lax.all_to_all(
            totals.reshape(LEVELS, 3, panels, half_count),
            "panel",
            split_axis=2,
            concat_axis=2,
            tiled=True,
        ),
    )
    merged = jnp.max(own_max, axis=2)
    totals = jnp.sum(own_tot * jnp.exp(own_max - merged[:, :, None, :]), axis=2)
    maxima = merged[:, 0, :]
    energy = maxima + jnp.log(totals[:, 0, :])
    matched = totals[:, 1:, :] / totals[:, 0:1, :]
    return (matched, energy)


def solution(mesh):
    placed = (P(("pairs", "blk", "panel"), None), P(("pairs", "blk"), None, "panel", None))
    return jax.shard_map(
        body,
        mesh=mesh,
        in_specs=placed,
        out_specs=(P(None, None, ("pairs", "blk", "panel")), P(None, ("pairs", "blk", "panel"))),
        check_vma=False,
    )
```

profile of v0, /device:TPU:0, one launch (start us, length us, event | category | flops | bytes accessed | tf_op | source)
XLA Modules:
  0.0 125.8 jit_solution(9972526232094171274)
XLA Ops:
  0.6 0.0 copy-start
  0.6 0.9 reshape.573
  1.5 0.0 copy-done
  1.5 0.0 copy-start.1
  1.5 32.7 %all_gather.15 = bf16[8,8,8,256]{3,2,1,0:T(8,128)(2,1)S(1)} all-gather(bf16[1,8,8,256]{3,2,1,0:T(8,128)(2,1)S(1)} %copy-done), channel_id=1, replica_groups=mesh['pairs'=2,'blk'=8,'panel'=2] {'blk'}, dimensions={0}, use_global_device_ids=true | all-gather | bytes 294912 | tf_op jit(solution)/shard_map/all_gather | solution.py:85
  34.2 0.0 copy-done.1
  34.2 1.9 %all_gather.16 = bf16[256,256]{1,0:T(8,128)(2,1)S(1)} all-gather(bf16[128,256]{1,0:T(8,128)(2,1)S(1)} %copy-done.1), channel_id=1, replica_groups=mesh['pairs'=2,'blk'=8,'panel'=2] {'panel'}, dimensions={0}, use_global_device_ids=true | all-gather | bytes 196608 | tf_op jit(solution)/shard_map/all_gather | solution.py:74
  36.1 0.1 reduce_sum.36
  36.2 30.5 %all-gather = bf16[32,4,256]{2,1,0:T(4,128)(2,1)S(1)} all-gather(bf16[4,4,256]{2,1,0:T(4,128)(2,1)S(1)} %get-tuple-element.6), channel_id=2, replica_groups=mesh['pairs'=2,'blk'=8,'panel'=2] {'blk'}, dimensions={0}, use_global_device_ids=true | all-gather | bytes 73728 | tf_op jit(solution)/shard_map/all_gather | solution.py:86
  66.7 0.2 fusion.48
  67.0 26.1 %all-gather.1 = bf16[16,2,256]{2,1,0:T(2,128)(2,1)S(1)} all-gather(bf16[2,2,256]{2,1,0:T(2,128)(2,1)S(1)} %get-tuple-element.8), channel_id=3, replica_groups=mesh['pairs'=2,'blk'=8,'panel'=2] {'blk'}, dimensions={0}, use_global_device_ids=true | all-gather | bytes 18432 | tf_op jit(solution)/shard_map/all_gather | solution.py:87
  93.2 0.2 fusion.47
  93.4 19.0 %all-gather.3 = bf16[8,1,256]{2,1,0:T(2,128)(2,1)S(1)} all-gather(bf16[1,1,256]{2,1,0:T(2,128)(2,1)S(1)} %reshape.580), channel_id=4, replica_groups=mesh['pairs'=2,'blk'=8,'panel'=2] {'blk'}, dimensions={0}, use_global_device_ids=true | all-gather | bytes 4608 | tf_op jit(solution)/shard_map/all_gather | solution.py:88
  112.4 0.2 fusion.46
  112.7 0.3 fusion.49
  113.0 0.6 pad_maximum_fusion.1
  113.6 3.2 %all-to-all-start.1 = ((f32[4,1,2,128]{3,0,1,2:T(4,128)}), f32[4,1,2,128]{3,0,1,2:T(4,128)S(1)}, u32[]{:S(2)}, u32[]{:S(2)}) async-start(f32[4,1,2,128]{3,0,1,2:T(4,128)} %pad_maximum_fusion.1), calls=%async_computation.1 | async-start | bytes 8192 | tf_op jit(solution)/shard_map/all_to_all | solution.py:98
  116.9 0.1 add_multiply_fusion.2
  117.0 0.1 mul.250
  117.1 0.1 add_multiply_fusion.3
  117.1 0.1 broadcast_in_dim.14
  117.2 0.1 mul.246
  117.4 0.2 convolution_add_fusion.2
  117.6 0.1 add_multiply_fusion
  117.7 0.1 mul.260
  117.8 0.1 add_multiply_fusion.1
  117.9 0.1 broadcast_in_dim.16
  118.0 0.1 mul.256
  118.1 0.2 convolution_add_fusion.1
  118.3 0.2 convolution_add_fusion
  118.5 0.1 add_multiply_fusion.4
  118.6 0.1 mul.239
  118.7 0.1 add_multiply_fusion.5
  118.8 0.1 broadcast_in_dim.12
  118.9 0.1 mul.234
  119.0 0.3 convolution_add_fusion.3
  119.3 0.1 stack.35
  119.4 0.6 pad_maximum_fusion
  120.0 0.0 all-to-all-done.1
  120.0 3.2 %all-to-all-start = ((f32[4,3,2,128]{3,0,1,2:T(4,128)}), f32[4,3,2,128]{3,0,1,2:T(4,128)S(1)}, u32[]{:S(2)}, u32[]{:S(2)}) async-start(f32[4,3,2,128]{3,0,1,2:T(4,128)} %pad_maximum_fusion), calls=%async_computation | async-start | bytes 24576 | tf_op jit(solution)/shard_map/all_to_all | solution.py:105
  123.3 1.3 %all-to-all-done = f32[4,3,2,128]{3,0,1,2:T(4,128)S(1)} async-done(((f32[4,3,2,128]{3,0,1,2:T(4,128)}), f32[4,3,2,128]{3,0,1,2:T(4,128)S(1)}, u32[]{:S(2)}, u32[]{:S(2)}) %all-to-all-start) | async-done | bytes 12320 | tf_op jit(solution)/shard_map/all_to_all | solution.py:105
  124.6 0.6 log_add_fusion
  125.2 0.6 copy_divide_fusion
  (35 shorter events, 0.3 us)
Async XLA Ops:
  0.6 0.9 copy-start
  1.5 32.7 %copy-start.1 = (bf16[128,256]{1,0:T(8,128)(2,1)S(1)}, bf16[128,256]{1,0:T(8,128)(2,1)}, u32[]{:S(2)}) copy-start(bf16[128,256]{1,0:T(8,128)(2,1)} %param.2) | copy-start | bytes 196612
  113.6 6.4 %all-to-all-start.1 = ((f32[4,1,2,128]{3,0,1,2:T(4,128)}), f32[4,1,2,128]{3,0,1,2:T(4,128)S(1)}, u32[]{:S(2)}, u32[]{:S(2)}) async-start(f32[4,1,2,128]{3,0,1,2:T(4,128)} %pad_maximum_fusion.1), calls=%async_computation.1 | async-start | bytes 8192 | tf_op jit(solution)/shard_map/all_to_all | solution.py:98
  120.0 4.6 %all-to-all-start = ((f32[4,3,2,128]{3,0,1,2:T(4,128)}), f32[4,3,2,128]{3,0,1,2:T(4,128)S(1)}, u32[]{:S(2)}, u32[]{:S(2)}) async-start(f32[4,3,2,128]{3,0,1,2:T(4,128)} %pad_maximum_fusion), calls=%async_computation | async-start | bytes 24576 | tf_op jit(solution)/shard_map/all_to_all | solution.py:105
where the time goes:
time: 126 us
  blocking collectives  110 us (87%)
  starting transfers between devices  6.45 us (5%)
  other arithmetic  3.09 us (2%)
  local copies, waits for them, and re-layouts  1.92 us (2%)
  matrix products  1.83 us (1%)
  waiting for transfers between devices  1.33 us (1%)
    all_gather x1, blocking collectives, body(): lax.all_gather(level_zero, 'blk', axis=0, tiled=True)  32.7 us
    all_gather x1, blocking collectives, body(): lax.all_gather(level_one, 'blk', axis=0, tiled=True)  30.5 us
    all_gather x1, blocking collectives, body(): lax.all_gather(level_two, 'blk', axis=0, tiled=True)  26.1 us
    all_gather x1, blocking collectives, body(): lax.all_gather(level_three, 'blk', axis=0, tiled=True)  19 us
    all_to_all x1, starting transfers between devices, body(): lax.all_to_all(totals.reshape(LEVELS, 3, panels, half_count), 'panel', sp...  3.23 us
    all_to_all x1, starting transfers between devices, body(): lax.all_to_all(maxima.reshape(LEVELS, 1, panels, half_count), 'panel', sp...  3.22 us
  transfers between devices with their start and end apart: 2, of which 1 were waited for; matrix products, arithmetic and copies ran while one was open for 2% of the time, Pallas kernels for 0%

commit v1 on v0

--- a/solution.py
+++ b/solution.py
@@ -8,6 +8,19 @@
 COLBLK = 8
 BCOLS = 16
 neg_large = -1e30
+
+
+def gather_around(x, axis, dim):
+    ways = lax.axis_size(axis)
+    up = [(d, (d + 1) % ways) for d in range(ways)]
+    down = [(d, (d - 1) % ways) for d in range(ways)]
+    earlier, later = ([x], [x])
+    for _ in range(ways // 2):
+        earlier.append(lax.ppermute(earlier[-1], axis, up))
+    for _ in range((ways - 1) // 2):
+        later.append(lax.ppermute(later[-1], axis, down))
+    line = jnp.concatenate([*earlier[::-1], *later[1:]], axis=dim)
+    return jnp.roll(line, (lax.axis_index(axis) - ways // 2) * x.shape[dim], axis=dim)
 
 
 def build_levels(tile_batch):
@@ -83,7 +96,7 @@
         list(
             (
                 lax.all_gather(level_zero, "blk", axis=0, tiled=True),
-                lax.all_gather(level_one, "blk", axis=0, tiled=True),
+                gather_around(level_one, "blk", 0),
                 lax.all_gather(level_two, "blk", axis=0, tiled=True),
                 lax.all_gather(level_three, "blk", axis=0, tiled=True),
             )

time: 126 us -> 119 us (0.944)
  blocking collectives: 110 us -> 77.1 us
  starting transfers between devices: 6.45 us -> 22.1 us
  waiting for transfers between devices: 1.33 us -> 11.2 us
    all_gather x1 -> x0, blocking collectives: 30.5 us -> none  [body(): lax.all_gather(level_one, 'blk', axis=0, tiled=True)]
    ppermute x0 -> x7, starting transfers between devices: none -> 15.7 us  [the longest x3 12.6 us: gather_around(): later.append(lax.ppermute(later[-1], axis, down))]
    ppermute x0 -> x7, waiting for transfers between devices: none -> 9.15 us  [the longest x4 8.97 us: gather_around(): earlier.append(lax.ppermute(earlier[-1], axis, up))]
    all_gather x1, blocking collectives: 32.7 us -> 30.9 us  [body(): lax.all_gather(level_zero, 'blk', axis=0, tiled=True)]
  transfers between devices with their start and end apart: 2 -> 9, of which waited for: 1 -> 6; matrix products, arithmetic and copies ran while one was open for 2% -> 3% of each run, Pallas kernels for 0% -> 0%
where the time goes in v1:
time: 119 us; the launch traced here: 118 us
  blocking collectives  77.1 us (65%)
  starting transfers between devices  22.1 us (19%)
  waiting for transfers between devices  11.2 us (9%)
  other arithmetic  3.13 us (3%)
  local copies, waits for them, and re-layouts  2.03 us (2%)
  matrix products  1.85 us (2%)
    all_gather x1, blocking collectives, body(): lax.all_gather(level_zero, 'blk', axis=0, tiled=True)  30.9 us
    all_gather x1, blocking collectives, body(): lax.all_gather(level_two, 'blk', axis=0, tiled=True)  26.1 us
    all_gather x1, blocking collectives, body(): lax.all_gather(level_three, 'blk', axis=0, tiled=True)  18.2 us
    ppermute x3, starting transfers between devices, gather_around(): later.append(lax.ppermute(later[-1], axis, down))  12.6 us
    ppermute x4, waiting for transfers between devices, gather_around(): earlier.append(lax.ppermute(earlier[-1], axis, up))  8.97 us
    all_to_all x1, starting transfers between devices, body(): lax.all_to_all(totals.reshape(LEVELS, 3, panels, half_count), 'panel', sp...  3.23 us
    all_to_all x1, starting transfers between devices, body(): lax.all_to_all(maxima.reshape(LEVELS, 1, panels, half_count), 'panel', sp...  3.22 us
    ppermute x4, starting transfers between devices, gather_around(): earlier.append(lax.ppermute(earlier[-1], axis, up))  3.08 us
  transfers between devices with their start and end apart: 9, of which 6 were waited for; matrix products, arithmetic and copies ran while one was open for 3% of the time, Pallas kernels for 0%

profile of v1, /device:TPU:0, one launch (start us, length us, event | category | flops | bytes accessed | tf_op | source)
XLA Modules:
  0.0 118.5 jit_solution(9881526643543207897)
XLA Ops:
  0.6 0.8 reshape.573
  1.4 0.1 reduce_sum.36
  1.5 3.0 %collective-permute-start = (bf16[1,4,4,256]{3,2,1,0:T(4,128)(2,1)S(1)}, bf16[1,4,4,256]{3,2,1,0:T(4,128)(2,1)S(1)}, u32[]{:S(2)}, u32[]{:S(2)}) collective-permute-start(bf16[1,4,4,256]{3,2,1,0:T(4,128)(2,1)S(1)} %get-tuple-element.6), channel_id=1, source_target_pairs={{0,2},{2,4},{4,6},{6,8},{8,10},{10,12},{12,14},{14,0},{1,3},{3,5},... | collective-permute-start | bytes 24584 | tf_op jit(solution)/shard_map/ppermute | solution.py:19
  4.5 3.1 %collective-permute-start.4 = (bf16[1,4,4,256]{3,2,1,0:T(4,128)(2,1)S(1)}, bf16[1,4,4,256]{3,2,1,0:T(4,128)(2,1)S(1)}, u32[]{:S(2)}, u32[]{:S(2)}) collective-permute-start(bf16[1,4,4,256]{3,2,1,0:T(4,128)(2,1)S(1)} %get-tuple-element.6), channel_id=1, source_target_pairs={{0,14},{2,0},{4,2},{6,4},{8,6},{10,8},{12,10},{14,12},{1,15},{3,1}... | collective-permute-start | bytes 24584 | tf_op jit(solution)/shard_map/ppermute | solution.py:21
  7.6 30.9 %all_gather.12 = bf16[8,8,8,256]{3,2,1,0:T(8,128)(2,1)S(1)} all-gather(bf16[1,8,8,256]{3,2,1,0:T(8,128)(2,1)S(1)} %copy-done), channel_id=1, replica_groups=mesh['pairs'=2,'blk'=8,'panel'=2] {'blk'}, dimensions={0}, use_global_device_ids=true | all-gather | bytes 294912 | tf_op jit(solution)/shard_map/all_gather | solution.py:98
  38.6 1.9 %all_gather.13 = bf16[256,256]{1,0:T(8,128)(2,1)S(1)} all-gather(bf16[128,256]{1,0:T(8,128)(2,1)S(1)} %copy-done.1), channel_id=1, replica_groups=mesh['pairs'=2,'blk'=8,'panel'=2] {'panel'}, dimensions={0}, use_global_device_ids=true | all-gather | bytes 196608 | tf_op jit(solution)/shard_map/all_gather | solution.py:87
  40.6 18.2 %all-gather.2 = bf16[8,1,256]{2,1,0:T(2,128)(2,1)S(1)} all-gather(bf16[1,1,256]{2,1,0:T(2,128)(2,1)S(1)} %reshape.578), channel_id=3, replica_groups=mesh['pairs'=2,'blk'=8,'panel'=2] {'blk'}, dimensions={0}, use_global_device_ids=true | all-gather | bytes 4608 | tf_op jit(solution)/shard_map/all_gather | solution.py:101
  58.8 0.2 fusion.45
  59.0 26.1 %all-gather = bf16[16,2,256]{2,1,0:T(2,128)(2,1)S(1)} all-gather(bf16[2,2,256]{2,1,0:T(2,128)(2,1)S(1)} %get-tuple-element.8), channel_id=2, replica_groups=mesh['pairs'=2,'blk'=8,'panel'=2] {'blk'}, dimensions={0}, use_global_device_ids=true | all-gather | bytes 18432 | tf_op jit(solution)/shard_map/all_gather | solution.py:100
  85.1 0.2 fusion.46
  85.4 0.1 add_multiply_fusion
  85.5 0.1 mul.260
  85.6 0.1 add_multiply_fusion.1
  85.6 0.1 broadcast_in_dim.16
  85.7 0.1 mul.256
  85.8 0.3 fusion.48
  86.1 0.1 add_multiply_fusion.4
  86.2 0.1 mul.239
  86.3 0.1 add_multiply_fusion.5
  86.4 0.1 broadcast_in_dim.12
  86.5 0.1 mul.234
  86.6 0.2 convolution_add_fusion
  86.8 0.2 convolution_add_fusion.1
  87.0 0.3 convolution_add_fusion.3
  87.3 0.1 multiply_add_fusion.1
  87.4 0.1 collective-permute-start.1
  87.4 0.1 add_multiply_fusion.2
  87.5 6.3 %collective-permute-done.1 = bf16[1,4,4,256]{3,2,1,0:T(4,128)(2,1)S(1)} collective-permute-done((bf16[1,4,4,256]{3,2,1,0:T(4,128)(2,1)S(1)}, bf16[1,4,4,256]{3,2,1,0:T(4,128)(2,1)S(1)}, u32[]{:S(2)}, u32[]{:S(2)}) %collective-permute-start.1) | collective-permute-done | bytes 8224 | tf_op jit(solution)/shard_map/ppermute | solution.py:19
  93.8 4.7 %collective-permute-start.5 = (bf16[1,4,4,256]{3,2,1,0:T(4,128)(2,1)S(1)}, bf16[1,4,4,256]{3,2,1,0:T(4,128)(2,1)S(1)}, u32[]{:S(2)}, u32[]{:S(2)}) collective-permute-start(bf16[1,4,4,256]{3,2,1,0:T(4,128)(2,1)S(1)} %collective-permute-done.4), channel_id=1, source_target_pairs={{0,14},{2,0},{4,2},{6,4},{8,6},{10,8},{12,10},{14,12},{1,15},{3,1}... | collective-permute-start | bytes 24584 | tf_op jit(solution)/shard_map/ppermute | solution.py:21
  98.5 1.6 %collective-permute-done.2 = bf16[1,4,4,256]{3,2,1,0:T(4,128)(2,1)S(1)} collective-permute-done((bf16[1,4,4,256]{3,2,1,0:T(4,128)(2,1)S(1)}, bf16[1,4,4,256]{3,2,1,0:T(4,128)(2,1)S(1)}, u32[]{:S(2)}, u32[]{:S(2)}) %collective-permute-start.2) | collective-permute-done | bytes 8224 | tf_op jit(solution)/shard_map/ppermute | solution.py:19
  100.1 0.1 add_multiply_fusion.3
  100.3 0.1 mul.250
  100.4 0.1 broadcast_in_dim.14
  100.5 0.1 mul.246
  100.6 0.0 collective-permute-done.5
  100.6 4.8 %collective-permute-start.6 = (bf16[1,4,4,256]{3,2,1,0:T(4,128)(2,1)S(1)}, bf16[1,4,4,256]{3,2,1,0:T(4,128)(2,1)S(1)}, u32[]{:S(2)}, u32[]{:S(2)}) collective-permute-start(bf16[1,4,4,256]{3,2,1,0:T(4,128)(2,1)S(1)} %collective-permute-done.5), channel_id=1, source_target_pairs={{0,14},{2,0},{4,2},{6,4},{8,6},{10,8},{12,10},{14,12},{1,15},{3,1}... | collective-permute-start | bytes 24584 | tf_op jit(solution)/shard_map/ppermute | solution.py:21
  105.4 1.1 collective-permute-done.3
  106.6 0.2 collective-permute-done.6
  107.0 0.2 fusion.47
  107.2 0.2 convolution_add_fusion.2
  107.4 0.6 pad_maximum_fusion.1
  108.1 3.2 %all-to-all-start.1 = ((f32[4,1,2,128]{3,0,1,2:T(4,128)}), f32[4,1,2,128]{3,0,1,2:T(4,128)S(1)}, u32[]{:S(2)}, u32[]{:S(2)}) async-start(f32[4,1,2,128]{3,0,1,2:T(4,128)} %pad_maximum_fusion.1), calls=%async_computation.1 | async-start | bytes 8192 | tf_op jit(solution)/shard_map/all_to_all | solution.py:111
  111.3 0.6 pad_maximum_fusion
  111.9 0.7 all-to-all-done.1
  112.6 3.2 %all-to-all-start = ((f32[4,3,2,128]{3,0,1,2:T(4,128)}), f32[4,3,2,128]{3,0,1,2:T(4,128)S(1)}, u32[]{:S(2)}, u32[]{:S(2)}) async-start(f32[4,3,2,128]{3,0,1,2:T(4,128)} %pad_maximum_fusion), calls=%async_computation | async-start | bytes 24576 | tf_op jit(solution)/shard_map/all_to_all | solution.py:118
  115.9 1.3 %all-to-all-done = f32[4,3,2,128]{3,0,1,2:T(4,128)S(1)} async-done(((f32[4,3,2,128]{3,0,1,2:T(4,128)}), f32[4,3,2,128]{3,0,1,2:T(4,128)S(1)}, u32[]{:S(2)}, u32[]{:S(2)}) %all-to-all-start) | async-done | bytes 12320 | tf_op jit(solution)/shard_map/all_to_all | solution.py:118
  117.3 0.6 log_add_fusion
  117.9 0.6 copy_divide_fusion
  (60 shorter events, 0.6 us)
Async XLA Ops:
  1.5 6.2 %copy-start = (bf16[1,8,8,256]{3,2,1,0:T(8,128)(2,1)S(1)}, bf16[1,8,8,256]{3,2,1,0:T(8,128)(2,1)}, u32[]{:S(2)}) copy-start(bf16[1,8,8,256]{3,2,1,0:T(8,128)(2,1)} %param.3) | copy-start | bytes 98308
  1.5 85.9 %collective-permute-start = (bf16[1,4,4,256]{3,2,1,0:T(4,128)(2,1)S(1)}, bf16[1,4,4,256]{3,2,1,0:T(4,128)(2,1)S(1)}, u32[]{:S(2)}, u32[]{:S(2)}) collective-permute-start(bf16[1,4,4,256]{3,2,1,0:T(4,128)(2,1)S(1)} %get-tuple-element.6), channel_id=1, source_target_pairs={{0,2},{2,4},{4,6},{6,8},{8,10},{10,12},{12,14},{14,0},{1,3},{3,5},... | collective-permute-start | bytes 24584 | tf_op jit(solution)/shard_map/ppermute | solution.py:19
  4.5 89.3 %collective-permute-start.4 = (bf16[1,4,4,256]{3,2,1,0:T(4,128)(2,1)S(1)}, bf16[1,4,4,256]{3,2,1,0:T(4,128)(2,1)S(1)}, u32[]{:S(2)}, u32[]{:S(2)}) collective-permute-start(bf16[1,4,4,256]{3,2,1,0:T(4,128)(2,1)S(1)} %get-tuple-element.6), channel_id=1, source_target_pairs={{0,14},{2,0},{4,2},{6,4},{8,6},{10,8},{12,10},{14,12},{1,15},{3,1}... | collective-permute-start | bytes 24584 | tf_op jit(solution)/shard_map/ppermute | solution.py:21
  7.6 30.9 %copy-start.1 = (bf16[128,256]{1,0:T(8,128)(2,1)S(1)}, bf16[128,256]{1,0:T(8,128)(2,1)}, u32[]{:S(2)}) copy-start(bf16[128,256]{1,0:T(8,128)(2,1)} %param.2) | copy-start | bytes 196612
  87.4 6.4 %collective-permute-start.1 = (bf16[1,4,4,256]{3,2,1,0:T(4,128)(2,1)S(1)}, bf16[1,4,4,256]{3,2,1,0:T(4,128)(2,1)S(1)}, u32[]{:S(2)}, u32[]{:S(2)}) collective-permute-start(bf16[1,4,4,256]{3,2,1,0:T(4,128)(2,1)S(1)} %collective-permute-done), channel_id=1, source_target_pairs={{0,2},{2,4},{4,6},{6,8},{8,10},{10,12},{12,14},{14,0},{1,3},{3,5},... | collective-permute-start | bytes 24584 | tf_op jit(solution)/shard_map/ppermute | solution.py:19
  93.8 6.3 %collective-permute-start.2 = (bf16[1,4,4,256]{3,2,1,0:T(4,128)(2,1)S(1)}, bf16[1,4,4,256]{3,2,1,0:T(4,128)(2,1)S(1)}, u32[]{:S(2)}, u32[]{:S(2)}) collective-permute-start(bf16[1,4,4,256]{3,2,1,0:T(4,128)(2,1)S(1)} %collective-permute-done.1), channel_id=1, source_target_pairs={{0,2},{2,4},{4,6},{6,8},{8,10},{10,12},{12,14},{14,0},{1,3},{3,5},... | collective-permute-start | bytes 24584 | tf_op jit(solution)/shard_map/ppermute | solution.py:19
  93.8 6.8 %collective-permute-start.5 = (bf16[1,4,4,256]{3,2,1,0:T(4,128)(2,1)S(1)}, bf16[1,4,4,256]{3,2,1,0:T(4,128)(2,1)S(1)}, u32[]{:S(2)}, u32[]{:S(2)}) collective-permute-start(bf16[1,4,4,256]{3,2,1,0:T(4,128)(2,1)S(1)} %collective-permute-done.4), channel_id=1, source_target_pairs={{0,14},{2,0},{4,2},{6,4},{8,6},{10,8},{12,10},{14,12},{1,15},{3,1}... | collective-permute-start | bytes 24584 | tf_op jit(solution)/shard_map/ppermute | solution.py:21
  100.1 6.3 %collective-permute-start.3 = (bf16[1,4,4,256]{3,2,1,0:T(4,128)(2,1)S(1)}, bf16[1,4,4,256]{3,2,1,0:T(4,128)(2,1)S(1)}, u32[]{:S(2)}, u32[]{:S(2)}) collective-permute-start(bf16[1,4,4,256]{3,2,1,0:T(4,128)(2,1)S(1)} %collective-permute-done.2), channel_id=1, source_target_pairs={{0,2},{2,4},{4,6},{6,8},{8,10},{10,12},{12,14},{14,0},{1,3},{3,5},... | collective-permute-start | bytes 24584 | tf_op jit(solution)/shard_map/ppermute | solution.py:19
  100.6 6.1 %collective-permute-start.6 = (bf16[1,4,4,256]{3,2,1,0:T(4,128)(2,1)S(1)}, bf16[1,4,4,256]{3,2,1,0:T(4,128)(2,1)S(1)}, u32[]{:S(2)}, u32[]{:S(2)}) collective-permute-start(bf16[1,4,4,256]{3,2,1,0:T(4,128)(2,1)S(1)} %collective-permute-done.5), channel_id=1, source_target_pairs={{0,14},{2,0},{4,2},{6,4},{8,6},{10,8},{12,10},{14,12},{1,15},{3,1}... | collective-permute-start | bytes 24584 | tf_op jit(solution)/shard_map/ppermute | solution.py:21
  108.1 4.6 %all-to-all-start.1 = ((f32[4,1,2,128]{3,0,1,2:T(4,128)}), f32[4,1,2,128]{3,0,1,2:T(4,128)S(1)}, u32[]{:S(2)}, u32[]{:S(2)}) async-start(f32[4,1,2,128]{3,0,1,2:T(4,128)} %pad_maximum_fusion.1), calls=%async_computation.1 | async-start | bytes 8192 | tf_op jit(solution)/shard_map/all_to_all | solution.py:111
  112.6 4.6 %all-to-all-start = ((f32[4,3,2,128]{3,0,1,2:T(4,128)}), f32[4,3,2,128]{3,0,1,2:T(4,128)S(1)}, u32[]{:S(2)}, u32[]{:S(2)}) async-start(f32[4,3,2,128]{3,0,1,2:T(4,128)} %pad_maximum_fusion), calls=%async_computation | async-start | bytes 24576 | tf_op jit(solution)/shard_map/all_to_all | solution.py:118
